TPU v7x, 32 devices: a whole 2x2x4 slice. The times are simulated.
32 devices in a mesh: rep: 8 (over z, x), grp: 4 (over y, core).
Axes of the slice: x: 2, y: 2, z: 4, core: 2. Of those that a mesh axis runs over, the one named last changes fastest.
Arguments:
- images: bfloat16 [32, 14, 14, 512], P(('rep', 'grp')), may hold values from -45 to 45
- cotangent: bfloat16 [32, 14, 14, 512], P(('rep', 'grp')), may hold values from -6 to 6
- region_ids: int32 [14, 14], replicated, may hold values from 0 to 8, as said below
- rel_index: int32 [169], replicated, may hold values from 0 to 168, each once
- matrices: float32 [3145728], P(('rep', 'grp')), may hold values from -0.8838835 to 0.8838835
- matrix_m: float32 [3145728], P(('rep', 'grp')), may hold values from -0.75 to 0.75
- matrix_v: float32 [3145728], P(('rep', 'grp')), may hold values from 2e-05 to 0.0005
- small: float32 [8848], replicated, may hold values from -4 to 301.5
- small_m: float32 [8848], replicated, may hold values from -0.75 to 0.75
- small_v: float32 [8848], replicated, may hold values from 2e-05 to 0.0005
Outputs:
- output: bfloat16 [32, 14, 14, 512], P(('rep', 'grp'))
- input_grad: bfloat16 [32, 14, 14, 512], P(('rep', 'grp'))
- matrix_grad: float32 [3145728], P(('rep', 'grp'))
- small_grad: float32 [8848], replicated
- new_matrices: float32 [3145728], P(('rep', 'grp'))
- new_matrix_m: float32 [3145728], P(('rep', 'grp'))
- new_matrix_v: float32 [3145728], P(('rep', 'grp'))
- new_small: float32 [8848], replicated
- new_small_m: float32 [8848], replicated
- new_small_v: float32 [8848], replicated
Inputs may be any that keep to these rules, and one draw needn't show every extreme that they name: `region_ids`: 3 times a row band plus a column band; each dimension is cut into three nonempty bands. `rel_index`: a permutation of the table's rows.
All inputs are finite; a program needn't handle non-finite values.
Results may differ from a plain program's by a relative error of at most 0.01.
The roundings to bfloat16 on the way count: a program that leaves them out, or rounds other values in their place, can miss the bound.
Values may be sent and summed in bfloat16 or wider, within the bound.
No kernel may reach another device: no remote copies, remote signals or barrier semaphores. Data moves between devices by JAX's collectives and lax.ppermute only.
A program may use at most 128 MiB of HBM per device.

v0:
```python
import math
import jax
import jax.numpy as jnp
from jax import lax
from jax.sharding import PartitionSpec as P

D = 512
HEADS = 16
FF = 2048
WIN = 7
SIDE = 14
SHIFT = 3
STEP = 5
HEAD_DIM = 32
REL = 169
norm_eps = 1e-05
beta_one = 0.9
beta_two = 0.999
adam_eps = 1e-08
rate_matrix = 0.01
rate_small = 0.2
decay_rate = 0.05
masked_score = -1e30
root_half = 0.7071067811865476
inv_root_twopi = 0.3989422804014327
highest = lax.Precision.HIGHEST


def norm_stats(values):
    center = values - jnp.mean(values, axis=-1, keepdims=True)
    spread = jnp.mean(center * center, axis=-1, keepdims=True)
    scaling = lax.rsqrt(spread + norm_eps)
    return (center * scaling, scaling)


def norm_back(incoming, normed, scaling, gain_vector):
    scaled = incoming * gain_vector
    backward = scaling * (
        scaled
        - jnp.mean(scaled, axis=-1, keepdims=True)
        - normed * jnp.mean(scaled * normed, axis=-1, keepdims=True)
    )
    return (backward, jnp.sum(incoming * normed, axis=(0, 1, 2)), jnp.sum(incoming, axis=(0, 1, 2)))


def gelu_slope(values):
    return (
        0.5 * (1.0 + lax.erf(values * root_half))
        + values * jnp.exp(-0.5 * values * values) * inv_root_twopi
    )


def to_windows(spatial):
    image_count = spatial.shape[0]
    blocks = SIDE // WIN
    rolled = jnp.roll(spatial, (-SHIFT, -SHIFT), axis=(1, 2))
    blocked = rolled.reshape(image_count, blocks, WIN, blocks, WIN, spatial.shape[-1])
    return blocked.transpose(0, 1, 3, 2, 4, 5).reshape(
        image_count, blocks * blocks, WIN * WIN, spatial.shape[-1]
    )


def from_windows(window_grid):
    image_count = window_grid.shape[0]
    blocks = SIDE // WIN
    blocked = window_grid.reshape(image_count, blocks, blocks, WIN, WIN, window_grid.shape[-1])
    spatial = blocked.transpose(0, 1, 3, 2, 4, 5).reshape(
        image_count, SIDE, SIDE, window_grid.shape[-1]
    )
    return jnp.roll(spatial, (SHIFT, SHIFT), axis=(1, 2))


def allowed_pairs(region_ids):
    blocks = SIDE // WIN
    window_grid = (
        region_ids.reshape(blocks, WIN, blocks, WIN)
        .transpose(0, 2, 1, 3)
        .reshape(blocks * blocks, WIN * WIN)
    )
    return window_grid[:, :, None] == window_grid[:, None, :]


def offset_grid():
    spots = jnp.arange(WIN * WIN, dtype=jnp.int32)
    rows_at = spots // WIN
    cols_at = spots % WIN
    return (rows_at[:, None] - rows_at[None, :] + WIN - 1) * (2 * WIN - 1) + (
        cols_at[:, None] - cols_at[None, :] + WIN - 1
    )


def lookup_tables(rel_index):
    labels = jnp.arange(REL, dtype=jnp.int32)
    select_offset = (offset_grid().reshape(-1)[:, None] == labels[None, :]).astype(jnp.float32)
    select_row = (rel_index[:, None] == labels[None, :]).astype(jnp.float32)
    return (select_offset, select_row)


def unpack_matrices(flat_weights):
    bound_one = 3 * D * D
    bound_two = bound_one + D * D
    bound_three = bound_two + D * FF
    return (
        flat_weights[:bound_one].reshape(D, 3 * D),
        flat_weights[bound_one:bound_two].reshape(D, D),
        flat_weights[bound_two:bound_three].reshape(D, FF),
        flat_weights[bound_three:].reshape(FF, D),
    )


def unpack_small(small):
    pieces = [small[number * D : (number + 1) * D] for number in range(8)]
    bias_up = small[8 * D : 8 * D + FF]
    rel_table = small[8 * D + FF :].reshape(REL, HEADS)
    return pieces + [bias_up, rel_table]


def adam_step(weights, first_moment, second_moment, gradient, rate, decay):
    new_first = beta_one * first_moment + (1.0 - beta_one) * gradient
    new_second = beta_two * second_moment + (1.0 - beta_two) * gradient * gradient
    first_hat = new_first / (1.0 - beta_one**STEP)
    second_hat = new_second / (1.0 - beta_two**STEP)
    update = first_hat / (jnp.sqrt(second_hat) + adam_eps) + decay * weights
    return (weights - rate * update, new_first, new_second)


def on_device(
    images, cotangent, region_ids, rel_index, matrices, matrix_m, matrix_v, small, small_m, small_v
):
    low_shard = matrices.astype(jnp.bfloat16)
    gathered = lax.all_gather(low_shard, ("rep", "grp"), axis=0, tiled=True)
    weight_qkv, weight_proj, weight_up, weight_down = unpack_matrices(gathered)
    small_parts = unpack_small(small)
    gain_one, gain_two, shift_one, bias_query, bias_value, bias_proj, shift_two, bias_down = (
        small_parts[:8]
    )
    bias_up = small_parts[8]
    image_count = images.shape[0]
    row_count = image_count * SIDE * SIDE
    places = WIN * WIN
    windows_count = (SIDE // WIN) ** 2
    score_scale = HEAD_DIM ** (-0.5)
    allowed = allowed_pairs(region_ids)[None, :, None]
    select_offset, select_row = lookup_tables(rel_index)
    table_rows = jnp.dot(select_row, small_parts[9], precision=highest)
    rel_bias = (
        jnp.dot(select_offset, table_rows, precision=highest)
        .reshape(places, places, HEADS)
        .transpose(2, 0, 1)
    )
    image_values = images.astype(jnp.float32)
    normed_one, scaling_one = norm_stats(image_values)
    input_one = (normed_one * gain_one + shift_one).astype(jnp.bfloat16)
    window_rows = to_windows(input_one).reshape(row_count, D)
    zeros_key = jnp.zeros((D,), jnp.float32)
    projected = jnp.dot(
        window_rows, weight_qkv, preferred_element_type=jnp.float32
    ) + jnp.concatenate([bias_query, zeros_key, bias_value])
    projected = projected.astype(jnp.bfloat16).reshape(
        image_count, windows_count, places, 3, HEADS, HEAD_DIM
    )
    queries = projected[:, :, :, 0]
    keys_part = projected[:, :, :, 1]
    values_part = projected[:, :, :, 2]

    def masked_scores():
        scores = (
            score_scale
            * jnp.einsum(
                "bnqhe,bnkhe->bnhqk", queries, keys_part, preferred_element_type=jnp.float32
            )
            + rel_bias
        )
        return jnp.where(allowed, scores, masked_score)

    masked = masked_scores()
    row_max = jnp.max(masked, axis=-1, keepdims=True)
    log_total = row_max + jnp.log(jnp.sum(jnp.exp(masked - row_max), axis=-1, keepdims=True))
    attention_low = jnp.exp(masked - log_total).astype(jnp.bfloat16)
    mixed_rows = jnp.einsum(
        "bnhqk,bnkhe->bnqhe", attention_low, values_part, preferred_element_type=jnp.float32
    )
    mixed_rows = mixed_rows.astype(jnp.bfloat16).reshape(row_count, D)
    attended = jnp.dot(mixed_rows, weight_proj, preferred_element_type=jnp.float32) + bias_proj
    resid_one = image_values + from_windows(attended.reshape(image_count, windows_count, places, D))
    normed_two, scaling_two = norm_stats(resid_one)
    input_two = (normed_two * gain_two + shift_two).astype(jnp.bfloat16).reshape(row_count, D)
    hidden_pre = jnp.dot(input_two, weight_up, preferred_element_type=jnp.float32) + bias_up
    hidden_act = jax.nn.gelu(hidden_pre, approximate=False).astype(jnp.bfloat16)
    result = resid_one + (
        jnp.dot(hidden_act, weight_down, preferred_element_type=jnp.float32) + bias_down
    ).reshape(image_count, SIDE, SIDE, D)
    output = result.astype(jnp.bfloat16)
    cot_rows = cotangent.reshape(row_count, D)
    grad_act = jnp.dot(cot_rows, weight_down.T, preferred_element_type=jnp.float32)
    down_grad = jnp.dot(hidden_act.T, cot_rows, preferred_element_type=jnp.float32)
    grad_pre = grad_act * gelu_slope(hidden_pre)
    pre_low = grad_pre.astype(jnp.bfloat16)
    up_grad = jnp.dot(input_two.T, pre_low, preferred_element_type=jnp.float32)
    grad_two = jnp.dot(pre_low, weight_up.T, preferred_element_type=jnp.float32).reshape(
        image_count, SIDE, SIDE, D
    )
    second_back, second_gain, second_shift = norm_back(grad_two, normed_two, scaling_two, gain_two)
    grad_resid = cotangent.astype(jnp.float32) + second_back
    grad_rows = to_windows(grad_resid.astype(jnp.bfloat16)).reshape(row_count, D)
    proj_grad = jnp.dot(mixed_rows.T, grad_rows, preferred_element_type=jnp.float32)
    mixed_grad = jnp.dot(grad_rows, weight_proj.T, preferred_element_type=jnp.float32).astype(
        jnp.bfloat16
    )
    mixed_grad = mixed_grad.reshape(image_count, windows_count, places, HEADS, HEAD_DIM)
    attention = jnp.exp(masked_scores() - log_total)
    attention_again = attention.astype(jnp.bfloat16)
    value_grad = jnp.einsum(
        "bnhqk,bnqhe->bnkhe", attention_again, mixed_grad, preferred_element_type=jnp.float32
    )
    prob_grad = jnp.einsum(
        "bnqhe,bnkhe->bnhqk", mixed_grad, values_part, preferred_element_type=jnp.float32
    )
    row_dot = jnp.sum(attention * prob_grad, axis=-1, keepdims=True)
    score_grad = attention * (prob_grad - row_dot)
    score_low = score_grad.astype(jnp.bfloat16)
    query_grad = score_scale * jnp.einsum(
        "bnhqk,bnkhe->bnqhe", score_low, keys_part, preferred_element_type=jnp.float32
    )
    key_grad = score_scale * jnp.einsum(
        "bnhqk,bnqhe->bnkhe", score_low, queries, preferred_element_type=jnp.float32
    )
    qkv_rows = (
        jnp.stack([query_grad, key_grad, value_grad], axis=3)
        .astype(jnp.bfloat16)
        .reshape(row_count, 3 * D)
    )
    qkv_grad = jnp.dot(window_rows.T, qkv_rows, preferred_element_type=jnp.float32)
    grad_one = from_windows(
        jnp.dot(qkv_rows, weight_qkv.T, preferred_element_type=jnp.float32).reshape(
            image_count, windows_count, places, D
        )
    )
    first_back, first_gain, first_shift = norm_back(grad_one, normed_one, scaling_one, gain_one)
    input_grad = (grad_resid + first_back).astype(jnp.bfloat16)
    rel_grad = jnp.sum(score_grad, axis=(0, 1)).transpose(1, 2, 0).reshape(places * places, HEADS)
    table_grad = jnp.dot(
        select_row.T, jnp.dot(select_offset.T, rel_grad, precision=highest), precision=highest
    )
    tokens_all = image_count * lax.axis_size("rep") * lax.axis_size("grp") * SIDE * SIDE
    grad_scale = 1.0 / math.sqrt(tokens_all)
    small_local = (
        jnp.concatenate(
            [
                first_gain,
                second_gain,
                first_shift,
                jnp.sum(query_grad, axis=(0, 1, 2)).reshape(D),
                jnp.sum(value_grad, axis=(0, 1, 2)).reshape(D),
                jnp.sum(grad_resid, axis=(0, 1, 2)),
                second_shift,
                jnp.sum(cot_rows, axis=0, dtype=jnp.float32),
                jnp.sum(grad_pre, axis=0),
                table_grad.reshape(-1),
            ]
        )
        * grad_scale
    )
    flat_grad = (
        jnp.concatenate(
            [
                qkv_grad.reshape(-1),
                proj_grad.reshape(-1),
                up_grad.reshape(-1),
                down_grad.reshape(-1),
            ]
        )
        * grad_scale
    )
    owned_grad = lax.psum_scatter(flat_grad, ("rep", "grp"), scatter_dimension=0, tiled=True)
    small_grad = lax.psum(small_local, ("rep", "grp"))
    new_matrices, new_matrix_m, new_matrix_v = adam_step(
        matrices, matrix_m, matrix_v, owned_grad, rate_matrix, decay_rate
    )
    new_small, new_small_m, new_small_v = adam_step(
        small, small_m, small_v, small_grad, rate_small, 0.0
    )
    return (
        output,
        input_grad,
        owned_grad,
        small_grad,
        new_matrices,
        new_matrix_m,
        new_matrix_v,
        new_small,
        new_small_m,
        new_small_v,
    )


def solution(mesh):
    in_specs = (
        P(("rep", "grp"), None, None, None),
        P(("rep", "grp"), None, None, None),
        P(),
        P(),
        P(("rep", "grp")),
        P(("rep", "grp")),
        P(("rep", "grp")),
        P(),
        P(),
        P(),
    )
    out_specs = (
        P(("rep", "grp"), None, None, None),
        P(("rep", "grp"), None, None, None),
        P(("rep", "grp")),
        P(),
        P(("rep", "grp")),
        P(("rep", "grp")),
        P(("rep", "grp")),
        P(),
        P(),
        P(),
    )
    return jax.shard_map(
        on_device, mesh=mesh, in_specs=in_specs, out_specs=out_specs, check_vma=False
    )
```

profile of v0, /device:TPU:0, one launch (start us, length us, event | category | flops | bytes accessed | tf_op | source)
XLA Modules:
  0.0 468.9 jit_solution(6778432741188791646)
XLA Ops:
  21.9 61.6 %all-gather.2.cloned.1.call-done = bf16[3145728]{0:T(1024)(128)(2,1)} async-done(((bf16[98304]{0:T(1024)(128)(2,1)}), bf16[3145728]{0:T(1024)(128)(2,1)}) %all-gather.2.cloned.1.call-update) | async-done | bytes 6291472 | tf_op jit(solution)/shard_map/all_gather | solution.py:131
  90.4 4.2 reshape.562
  94.6 3.1 fusion.71
  97.7 2.6 copy.135
  116.6 4.5 fusion.70
  121.1 4.4 slice.182
  128.3 2.8 convert_reduce_fusion
  132.7 4.6 slice.179
  137.3 6.9 %fusion.5 = (bf16[196,2048]{1,0:T(8,128)(2,1)S(1)}, f32[196,2048]{1,0:T(8,128)}) fusion(f32[2048]{0:T(1024)S(1)} %slice-done, bf16[196,512]{1,0:T(8,128)(2,1)} %reshape.543, bf16[512,2048]{1,0:T(8,128)(2,1)} %slice.179), kind=kOutput, calls=%fused_computation.20 | convolution fusion | flops 437534720 | bytes 4714496 | tf_op jit(solution)/shard_map/dot_general | solution.py:188
  146.5 2.2 reshape.559
  148.7 3.3 fusion.74
  153.7 2.3 reshape.563
  156.0 4.2 multiply_reduce_fusion.2
  160.2 3.9 fusion.65
  174.8 2.4 convolution_bitcast_fusion.2
  177.2 2.3 reshape.564
  179.5 2.6 copy.105
  187.6 2.7 convolution_bitcast_fusion
  190.3 2.7 convolution_bitcast_fusion.1
  194.7 2.4 copy.113
  197.2 3.5 convert_element_type.105
  200.7 3.5 fusion.75
  204.2 4.5 reshape.550
  208.8 3.4 copy.139
  214.4 15.5 %maximum_multiply_fusion = f32[3145728]{0:T(1024)} fusion(f32[1048576]{0:T(1024)S(1)} %bitcast.114, f32[1048576]{0:T(1024)S(1)} %bitcast.115, f32[262144]{0:T(1024)S(1)} %bitcast.116, f32[786432]{0:T(1024)S(1)} %copy-done.1), kind=kLoop, calls=%fused_computation | loop fusion | flops 12582912 | bytes 25165824 | tf_op jit(solution)/shard_map/mul | solution.py:265
  229.9 2.7 reshape.558
  232.6 3.4 copy.125
  236.0 4.1 reshape.560
  245.1 5.4 %multiply_reduce_fusion.3 = (f32[512]{0:T(512)S(1)}, f32[14,14]{1,0:T(8,128)S(1)}, f32[14,14]{1,0:T(8,128)S(1)}, f32[1,14,14,512]{3,0,2,1:T(1,128)S(1)}) fusion(f32[14,14]{1,0:T(8,128)S(1)} %add_rsqrt_fusion.1, f32[14,14]{1,0:T(8,128)S(1)} %broadcast_multiply_fusion.6, bf16[1,14,14,512]{3,2,1,0:T(8,128)(2,1)S(1)} %copy-done.4, f32[512]{0:T(512)S(1)} %copy-done.36, ...), kind=kLoop, calls=%fused_computation.87 | loop fusion | flops 1002616 | bytes 1010752 | tf_op jit(solution)/shard_map/reduce_sum | solution.py:43
  252.8 41.0 %psum.7 = f32[8848]{0:T(1024)S(1)} all-reduce(f32[8848]{0:T(1024)S(1)} %broadcast_multiply_fusion.1), channel_id=1, replica_groups=mesh['rep'=8,'grp'=4] {'rep','grp'}, use_global_device_ids=true, to_apply=%region_23.24 | all-reduce | flops 8848 | bytes 70784 | tf_op jit(solution)/shard_map/psum | solution.py:276
  294.5 164.9 %all-reduce.3.cloned.1.call-done = f32[3145728]{0:T(1024)} async-done(((f32[3145728]{0:T(1024)}), f32[3145728]{0:T(1024)}) %all-reduce.3.cloned.1.call-update) | async-done | bytes 12582928
  459.4 2.2 multiply_subtract_fusion
  (199 shorter events, 73.7 us)
Async XLA Ops:
  7.2 9.4 %slice-start.1 = ((f32[8848]{0:T(1024)}), f32[2704]{0:T(1024)S(1)}, s32[]{:S(2)}) async-start(f32[8848]{0:T(1024)} %param.17), calls=%async_computation.3 | async-start | bytes 24576 | tf_op jit(solution)/shard_map/slice | solution.py:114
  7.2 9.0 %copy-start.39 = (s32[14,14]{1,0:T(8,128)S(1)}, s32[14,14]{1,0:T(8,128)}, u32[]{:S(2)}) copy-start(s32[14,14]{1,0:T(8,128)} %param.12) | copy-start | bytes 2356
  7.2 9.5 %copy-start.26 = (bf16[1,14,14,512]{3,2,1,0:T(8,128)(2,1)S(1)}, bf16[1,14,14,512]{3,2,1,0:T(8,128)(2,1)}, u32[]{:S(2)}) copy-start(bf16[1,14,14,512]{3,2,1,0:T(8,128)(2,1)} %param.11) | copy-start | bytes 602116
  7.2 10.2 %copy-start.40 = (s32[169]{0:T(256)S(1)}, s32[169]{0:T(256)}, u32[]{:S(2)}) copy-start(s32[169]{0:T(256)} %param.13) | copy-start | bytes 2032
  7.2 76.3 %all-gather.2.cloned.1.call-start = ((), (), s32[]{:S(2)}) async-start(), calls=%async_computation | async-start | bytes 6488064 | tf_op jit(solution)/shard_map/all_gather | solution.py:131
  9.1 450.4 %all-reduce.3.cloned.1.call-start = ((), (), s32[]{:S(2)}) async-start(), calls=%async_computation.1 | async-start | bytes 25165824
  16.6 4.0 copy-start.37
  21.8 67.3 %copy-start.19 = (bf16[196,512]{1,0:T(8,128)(2,1)}, bf16[196,512]{1,0:T(8,128)(2,1)S(1)}, u32[]{:S(2)}) copy-start(bf16[196,512]{1,0:T(8,128)(2,1)S(1)} %reshape_reshape.10) | copy-start | bytes 602116
  121.1 7.2 %copy-start.32 = (f32[512]{0:T(512)S(1)}, f32[512]{0:T(512)}, u32[]{:S(2)}) copy-start(f32[512]{0:T(512)} %get-tuple-element.74) | copy-start | bytes 6148
  132.7 4.6 slice-start
  137.3 7.8 %copy-start.18 = (bf16[2048,512]{1,0:T(8,128)(2,1)S(1)}, bf16[2048,512]{1,0:T(8,128)(2,1)}, u32[]{:S(2)}) copy-start(bf16[2048,512]{1,0:T(8,128)(2,1)} %slice.182) | copy-start | bytes 6291460
  137.3 7.8 %copy-start.42 = (f32[512]{0:T(512)S(1)}, f32[512]{0:T(512)}, u32[]{:S(2)}) copy-start(f32[512]{0:T(512)} %get-tuple-element.72) | copy-start | bytes 6148
  148.7 3.3 copy-start.3
  187.6 2.7 copy-start.15
  187.6 2.7 copy-start.25
  190.3 2.7 copy-start.11
  197.2 3.5 copy-start.20
  208.7 3.5 copy-start
  212.2 1.9 copy-start.1
  212.2 2.2 copy-start.10
  236.0 4.1 copy-start.23
  241.4 2.5 copy-start.41
  242.5 2.5 copy-start.4
  242.5 2.5 copy-start.36
  242.9 7.6 %copy-start.13 = (f32[1,14,14,512]{3,0,2,1:T(1,128)S(1)}, f32[1,14,14,512]{3,0,2,1:T(1,128)}, u32[]{:S(2)}) copy-start(f32[1,14,14,512]{3,0,2,1:T(1,128)} %copy-done.12) | copy-start | bytes 1204228
  245.0 48.8 %copy-start.30 = (f32[8848]{0:T(1024)S(1)}, f32[8848]{0:T(1024)}, u32[]{:S(2)}) copy-start(f32[8848]{0:T(1024)} %param.17) | copy-start | bytes 106180
  245.0 48.8 %copy-start.33 = (f32[8848]{0:T(1024)S(1)}, f32[8848]{0:T(1024)}, u32[]{:S(2)}) copy-start(f32[8848]{0:T(1024)} %param.18) | copy-start | bytes 106180
  245.0 48.8 %copy-start.34 = (f32[8848]{0:T(1024)S(1)}, f32[8848]{0:T(1024)}, u32[]{:S(2)}) copy-start(f32[8848]{0:T(1024)} %param.19) | copy-start | bytes 106180
  245.1 214.4 %copy-start.24 = (f32[98304]{0:T(1024)S(1)}, f32[98304]{0:T(1024)}, u32[]{:S(2)}) copy-start(f32[98304]{0:T(1024)} %param.14) | copy-start | bytes 1179652
  245.1 214.3 %copy-start.28 = (f32[98304]{0:T(1024)S(1)}, f32[98304]{0:T(1024)}, u32[]{:S(2)}) copy-start(f32[98304]{0:T(1024)} %param.15) | copy-start | bytes 1179652
  245.1 214.3 %copy-start.29 = (f32[98304]{0:T(1024)S(1)}, f32[98304]{0:T(1024)}, u32[]{:S(2)}) copy-start(f32[98304]{0:T(1024)} %param.16) | copy-start | bytes 1179652
  293.8 167.8 %copy-start.31 = (f32[8848]{0:T(1024)}, f32[8848]{0:T(1024)S(1)}, u32[]{:S(2)}) copy-start(f32[8848]{0:T(1024)S(1)} %psum.7) | copy-start | bytes 106180
  (15 other events, 20.8 us)
Sparse Core Ops, SparseCore 0:
  11.5 71.9 all-gather.1
  230.0 229.3 all-reduce.2
where the time goes:
time: 477 us; the launch traced here: 469 us
  waiting for transfers between devices  227 us (48%)
  local copies, waits for them, and re-layouts  93.5 us (20%)
  other arithmetic  52.5 us (11%)
  blocking collectives  41 us (9%)
  matrix products  39.9 us (8%)
  between operations  15.4 us (3%)
    unnamed x3, waiting for transfers between devices  165 us
    all_gather x1, waiting for transfers between devices, on_device(): gathered = lax.all_gather(low_shard, ('rep', 'grp'), axis=0, tiled=True)  61.6 us
    psum x1, blocking collectives, on_device(): small_grad = lax.psum(small_local, ('rep', 'grp'))  41 us
    unnamed x102, local copies, waits for them, and re-layouts  16.9 us
    mul x1, other arithmetic, on_device(): jnp.concatenate([qkv_grad.reshape(-1), proj_grad.reshape(-1), up_grad.res...  15.5 us
    convert_element_type x4, local copies, waits for them, and re-layouts, on_device(): qkv_rows = jnp.stack([query_grad, key_grad, value_grad], axis=3).astype(j...  13.5 us
    reduce_sum x2, other arithmetic, norm_back(): jnp.sum(incoming * normed, axis=(0, 1, 2))  9.56 us
  transfers between devices with their start and end apart: 2, of which 2 were waited for; matrix products, arithmetic and copies ran while one was open for 8% of the time, Pallas kernels for 0%

commit v1 on v0

--- a/solution.py
+++ b/solution.py
@@ -273,7 +273,12 @@
         * grad_scale
     )
     owned_grad = lax.psum_scatter(flat_grad, ("rep", "grp"), scatter_dimension=0, tiled=True)
-    small_grad = lax.psum(small_local, ("rep", "grp"))
+
+    def link_boxes(tile_in):
+        local_now = lax.all_gather(tile_in, axis_name=("rep", "grp"))
+        return jnp.sum(local_now, 0)
+
+    small_grad = link_boxes(small_local)
     new_matrices, new_matrix_m, new_matrix_v = adam_step(
         matrices, matrix_m, matrix_v, owned_grad, rate_matrix, decay_rate
     )

time: 477 us -> 507 us (1.063)
  waiting for transfers between devices: 227 us -> 318 us
  blocking collectives: 41 us -> 0 us
  local copies, waits for them, and re-layouts: 93.5 us -> 75 us
    unnamed x3 -> x4, waiting for transfers between devices: 165 us -> 233 us
    psum x1 -> x0, blocking collectives: 41 us -> none  [on_device(): small_grad = lax.psum(small_local, ('rep', 'grp'))]
    all_gather x0 -> x1, waiting for transfers between devices: none -> 23.1 us  [link_boxes(): local_now = lax.all_gather(tile_in, axis_name=('rep', 'grp'))]
    unnamed x102 -> x111, local copies, waits for them, and re-layouts: 16.9 us -> 16 us
  transfers between devices with their start and end apart: 2 -> 3, of which waited for: 2 -> 3; matrix products, arithmetic and copies ran while one was open for 8% -> 9% of each run, Pallas kernels for 0% -> 0%
where the time goes in v1:
time: 507 us; the launch traced here: 498 us
  waiting for transfers between devices  318 us (63%)
  local copies, waits for them, and re-layouts  75 us (15%)
  other arithmetic  54.9 us (11%)
  matrix products  35.1 us (7%)
  between operations  15.1 us (3%)
    unnamed x4, waiting for transfers between devices  233 us
    all_gather x1, waiting for transfers between devices, on_device(): gathered = lax.all_gather(low_shard, ('rep', 'grp'), axis=0, tiled=True)  62.2 us
    all_gather x1, waiting for transfers between devices, link_boxes(): local_now = lax.all_gather(tile_in, axis_name=('rep', 'grp'))  23.1 us
    unnamed x111, local copies, waits for them, and re-layouts  16 us
    mul x1, other arithmetic, on_device(): jnp.concatenate([qkv_grad.reshape(-1), proj_grad.reshape(-1), up_grad.res...  15.5 us
    convert_element_type x4, local copies, waits for them, and re-layouts, on_device(): qkv_rows = jnp.stack([query_grad, key_grad, value_grad], axis=3).astype(j...  10.3 us
  transfers between devices with their start and end apart: 3, of which 3 were waited for; matrix products, arithmetic and copies ran while one was open for 9% of the time, Pallas kernels for 0%

profile of v1, /device:TPU:0, one launch (start us, length us, event | category | flops | bytes accessed | tf_op | source)
XLA Modules:
  0.0 498.2 jit_solution(9530544378631424900)
XLA Ops:
  10.7 1.9 multiply_reduce_fusion.7
  21.3 62.2 %all-gather.4.cloned.1.call-done = bf16[3145728]{0:T(1024)(128)(2,1)} async-done(((bf16[98304]{0:T(1024)(128)(2,1)}), bf16[3145728]{0:T(1024)(128)(2,1)}) %all-gather.4.cloned.1.call-update) | async-done | bytes 6291472 | tf_op jit(solution)/shard_map/all_gather | solution.py:131
  85.0 2.7 reshape.687
  93.0 3.2 reshape.691
  97.8 1.9 copy.135
  99.7 2.0 copy.134
  102.5 1.9 fusion.73
  109.2 4.5 fusion.70
  113.7 4.4 slice.182
  119.8 2.1 convert_reduce_fusion
  122.9 4.6 slice.179
  127.5 6.8 %fusion.5 = (bf16[196,2048]{1,0:T(8,128)(2,1)S(1)}, f32[196,2048]{1,0:T(8,128)}) fusion(f32[2048]{0:T(1024)S(1)} %slice-done, bf16[196,512]{1,0:T(8,128)(2,1)S(1)} %reshape.673, bf16[512,2048]{1,0:T(8,128)(2,1)} %slice.179), kind=kOutput, calls=%fused_computation.20 | convolution fusion | flops 437534720 | bytes 4714496 | tf_op jit(solution)/shard_map/dot_general | solution.py:188
  136.6 2.3 reshape.688
  138.8 3.3 fusion.74
  143.8 2.3 reshape.692
  146.0 4.1 multiply_reduce_fusion.2
  150.1 5.0 %fusion.65 = (f32[512]{0:T(512)}, f32[1,14,14,512]{3,0,2,1:T(1,128)S(1)}, bf16[1,14,14,512]{3,0,2,1:T(2,128)(2,1)}, f32[512]{0:T(512)}) fusion(f32[14,14]{1,0:T(8,128)S(1)} %broadcast_multiply_fusion.3, f32[1,14,14,512]{3,0,2,1:T(1,128)S(1)} %get-tuple-element.64, f32[14,14]{1,0:T(8,128)S(1)} %broadcast_multiply_fusion.4, f32[14,14]{1,0:T(8,128)S(1)} %div.78, ...), kind=kLoop, calls=%fused_computation.154 | loop fusion | flops 1303552 | bytes 2016320 | tf_op jit(solution)/shard_map/reduce_sum | solution.py:255
  165.2 1.8 copy.105
  173.4 3.4 copy.125
  176.8 4.8 reshape.689
  181.6 1.9 fusion.24
  184.8 2.7 convolution_bitcast_fusion
  187.5 2.7 convolution_bitcast_fusion.1
  194.4 5.9 %multiply_reduce_fusion.3 = (f32[512]{0:T(512)S(1)}, f32[14,14]{1,0:T(8,128)S(1)}, f32[14,14]{1,0:T(8,128)S(1)}, f32[1,14,14,512]{3,0,2,1:T(1,128)}) fusion(f32[14,14]{1,0:T(8,128)S(1)} %add_rsqrt_fusion.1, f32[14,14]{1,0:T(8,128)S(1)} %broadcast_multiply_fusion.5, bf16[1,14,14,512]{3,2,1,0:T(8,128)(2,1)S(1)} %copy-done.2, f32[512]{0:T(512)S(1)} %get-tuple-element.79, ...), kind=kLoop, calls=%fused_computation.87 | loop fusion | flops 1002616 | bytes 1010752 | tf_op jit(solution)/shard_map/reduce_sum | solution.py:43
  201.2 2.4 fusion.75
  203.6 2.9 reshape.680
  206.5 3.5 copy.139
  211.2 15.5 %maximum_multiply_fusion = f32[3145728]{0:T(1024)} fusion(f32[1048576]{0:T(1024)S(1)} %bitcast.123, f32[1048576]{0:T(1024)S(1)} %bitcast.124, f32[262144]{0:T(1024)S(1)} %bitcast.125, f32[786432]{0:T(1024)S(1)} %reshape.680), kind=kLoop, calls=%fused_computation | loop fusion | flops 12582912 | bytes 25165824 | tf_op jit(solution)/shard_map/mul | solution.py:265
  230.7 23.1 %all-gather.6.cloned.1.call-done = f32[32,1,8848]{2,1,0:T(1,128)} async-done(((f32[1,1,8848]{2,1,0:T(1,128)}), f32[32,1,8848]{2,1,0:T(1,128)}) %all-gather.6.cloned.1.call-update) | async-done | bytes 1132560 | tf_op jit(solution)/shard_map/all_gather | solution.py:278
  253.7 1.9 reduce_sum.225
  256.4 232.6 %all-reduce.3.cloned.1.call-done = f32[3145728]{0:T(1024)} async-done(((f32[3145728]{0:T(1024)}), f32[3145728]{0:T(1024)}) %all-reduce.3.cloned.1.call-update) | async-done | bytes 12582928
  489.0 2.2 multiply_subtract_fusion
  (210 shorter events, 60.8 us)
Async XLA Ops:
  7.2 8.8 %slice-start.1 = ((f32[8848]{0:T(1024)}), f32[2704]{0:T(1024)S(1)}, s32[]{:S(2)}) async-start(f32[8848]{0:T(1024)} %param.17), calls=%async_computation.4 | async-start | bytes 24576 | tf_op jit(solution)/shard_map/slice | solution.py:114
  7.2 8.4 %copy-start.42 = (s32[14,14]{1,0:T(8,128)S(1)}, s32[14,14]{1,0:T(8,128)}, u32[]{:S(2)}) copy-start(s32[14,14]{1,0:T(8,128)} %param.12) | copy-start | bytes 2356
  7.2 8.9 %copy-start.31 = (bf16[1,14,14,512]{3,2,1,0:T(8,128)(2,1)S(1)}, bf16[1,14,14,512]{3,2,1,0:T(8,128)(2,1)}, u32[]{:S(2)}) copy-start(bf16[1,14,14,512]{3,2,1,0:T(8,128)(2,1)} %param.11) | copy-start | bytes 602116
  7.2 9.6 %copy-start.45 = (s32[169]{0:T(256)S(1)}, s32[169]{0:T(256)}, u32[]{:S(2)}) copy-start(s32[169]{0:T(256)} %param.13) | copy-start | bytes 2032
  7.2 76.3 %all-gather.4.cloned.1.call-start = ((), (), s32[]{:S(2)}) async-start(), calls=%async_computation | async-start | bytes 6488064 | tf_op jit(solution)/shard_map/all_gather | solution.py:131
  9.1 244.7 %all-gather.6.cloned.1.call-start = ((), (), s32[]{:S(2)}) async-start(), calls=%async_computation.1 | async-start | bytes 1182720 | tf_op jit(solution)/shard_map/all_gather | solution.py:278
  21.2 70.5 %copy-start.22 = (bf16[196,512]{1,0:T(8,128)(2,1)}, bf16[196,512]{1,0:T(8,128)(2,1)S(1)}, u32[]{:S(2)}) copy-start(bf16[196,512]{1,0:T(8,128)(2,1)S(1)} %reshape_reshape.10) | copy-start | bytes 602116
  97.8 3.9 copy-start.16
  99.7 4.7 copy-start.6
  101.7 3.2 copy-start.4
  106.1 3.1 copy-start.19
  113.7 4.4 copy-start.2
  122.8 4.7 copy-start.29
  122.8 4.7 slice-start
  127.5 7.7 %copy-start.21 = (bf16[2048,512]{1,0:T(8,128)(2,1)S(1)}, bf16[2048,512]{1,0:T(8,128)(2,1)}, u32[]{:S(2)}) copy-start(bf16[2048,512]{1,0:T(8,128)(2,1)} %slice.182) | copy-start | bytes 6291460
  135.2 3.6 copy-start.34
  138.8 3.3 copy-start.1
  143.7 6.4 %copy-start.32 = (bf16[1,14,14,512]{3,2,1,0:T(8,128)(2,1)S(1)}, bf16[1,14,14,512]{3,2,1,0:T(8,128)(2,1)}, u32[]{:S(2)}) copy-start(bf16[1,14,14,512]{3,2,1,0:T(8,128)(2,1)} %param.11) | copy-start | bytes 602116
  157.1 5.4 %copy-start.20 = (bf16[196,512]{0,1:T(8,128)(2,1)S(1)}, bf16[196,512]{0,1:T(8,128)(2,1)}, u32[]{:S(2)}) copy-start(bf16[196,512]{0,1:T(8,128)(2,1)} %copy-done.19) | copy-start | bytes 602116
  176.8 4.8 copy-start.27
  193.5 6.9 %copy-start.44 = (f32[512]{0:T(512)S(1)}, f32[512]{0:T(512)}, u32[]{:S(2)}) copy-start(f32[512]{0:T(512)} %get-tuple-element.56) | copy-start | bytes 6148
  193.5 6.9 %copy-start.43 = (f32[512]{0:T(512)S(1)}, f32[512]{0:T(512)}, u32[]{:S(2)}) copy-start(f32[512]{0:T(512)} %get-tuple-element.71) | copy-start | bytes 6148
  193.5 7.7 %copy-start.23 = (bf16[196,512]{1,0:T(8,128)(2,1)S(1)}, bf16[196,512]{1,0:T(8,128)(2,1)}, u32[]{:S(2)}) copy-start(bf16[196,512]{1,0:T(8,128)(2,1)} %copy-done.22) | copy-start | bytes 602116
  201.2 287.8 %all-reduce.3.cloned.1.call-start = ((), (), s32[]{:S(2)}) async-start(), calls=%async_computation.2 | async-start | bytes 25165824
  206.5 3.5 copy-start
  228.4 27.2 %copy-start.39 = (f32[8848]{0:T(1024)S(1)}, f32[8848]{0:T(1024)}, u32[]{:S(2)}) copy-start(f32[8848]{0:T(1024)} %param.17) | copy-start | bytes 106180
  228.4 27.2 %copy-start.40 = (f32[8848]{0:T(1024)S(1)}, f32[8848]{0:T(1024)}, u32[]{:S(2)}) copy-start(f32[8848]{0:T(1024)} %param.18) | copy-start | bytes 106180
  228.5 27.2 %copy-start.41 = (f32[8848]{0:T(1024)S(1)}, f32[8848]{0:T(1024)}, u32[]{:S(2)}) copy-start(f32[8848]{0:T(1024)} %param.19) | copy-start | bytes 106180
  228.5 260.5 %copy-start.28 = (f32[98304]{0:T(1024)S(1)}, f32[98304]{0:T(1024)}, u32[]{:S(2)}) copy-start(f32[98304]{0:T(1024)} %param.14) | copy-start | bytes 1179652
  228.5 260.5 %copy-start.36 = (f32[98304]{0:T(1024)S(1)}, f32[98304]{0:T(1024)}, u32[]{:S(2)}) copy-start(f32[98304]{0:T(1024)} %param.15) | copy-start | bytes 1179652
  228.5 260.5 %copy-start.37 = (f32[98304]{0:T(1024)S(1)}, f32[98304]{0:T(1024)}, u32[]{:S(2)}) copy-start(f32[98304]{0:T(1024)} %param.16) | copy-start | bytes 1179652
  255.7 235.5 %copy-start.38 = (f32[8848]{0:T(1024)}, f32[8848]{0:T(1024)S(1)}, u32[]{:S(2)}) copy-start(f32[8848]{0:T(1024)S(1)} %reduce_sum.225) | copy-start | bytes 106180
  (20 other events, 30.4 us)
Sparse Core Ops, SparseCore 0:
  11.5 71.9 all-gather.3
  201.3 52.4 all-gather.5
  259.8 229.1 all-reduce.2
